TPU v7x, 1024 devices: a whole 8x8x8 slice. The times are simulated.
1024 devices in a mesh: ctx: 64 (over x, z), tp: 16 (over y, core).
Axes of the slice: x: 8, y: 8, z: 8, core: 2. Of those that a mesh axis runs over, the one named last changes fastest.
Arguments:
- queries: bfloat16 [16384, 4096], P('ctx', 'tp'), may hold values from -6 to 6
- keys: bfloat16 [16384, 2048], P('ctx', 'tp'), may hold values from -6 to 6
- values: bfloat16 [16384, 2048], P('ctx', 'tp'), may hold values from -6 to 6
- out_weight: bfloat16 [4096, 2688], P('tp'), may hold values from -0.09375 to 0.09375
- out_grad: bfloat16 [16384, 2688], P('ctx'), may hold values from -16 to 16
- block_doc: int32 [64], replicated, may hold values from 0 to 15, never falling along the last dimension, each value on 1 to 10 neighbouring positions
Outputs:
- attn_output: bfloat16 [16384, 2688], P('ctx', 'tp')
- query_grad: bfloat16 [16384, 4096], P('ctx', 'tp')
- key_grad: bfloat16 [16384, 2048], P('ctx', 'tp')
- value_grad: bfloat16 [16384, 2048], P('ctx', 'tp')
- out_weight_grad: float32 [4096, 2688], P('tp', 'ctx')
Inputs may be any that keep to these rules, and one draw needn't show every extreme that they name: block_doc never falls; each document covers 1 to 10 whole blocks, one exactly 10.
All inputs are finite; a program needn't handle non-finite values.
Results may differ from a plain program's by a relative error of at most 0.017.
Values may be sent and summed in bfloat16 or wider, within the bound.
A program may use at most 64 MiB of HBM per device.

v0:
```python
import jax
import jax.numpy as jnp
from jax import lax
from jax.sharding import PartitionSpec as P

HEAD = 128
WINDOW = 1024


query_scale = 168.0 ** (-0.5)


def shifted(shard, axis, by):
    size = lax.axis_size(axis)
    pairs = [(i, i + by) for i in range(size) if 0 <= i + by < size]
    return lax.ppermute(shard, axis, pairs)


def local(queries, keys, values, out_weight, out_grad, block_doc):
    tok_rows = queries.shape[0]
    head_size = HEAD
    kv_count = keys.shape[1] // head_size
    group_size = queries.shape[1] // keys.shape[1]
    key_width = keys.shape[1]
    span_blocks = WINDOW // tok_rows
    reach_blocks = min(span_blocks, lax.axis_size("ctx") - 1)
    own_block = lax.axis_index("ctx")
    paired = jnp.stack([keys, values])
    by_distance = jnp.stack(
        [paired] + [shifted(paired, "ctx", distance) for distance in range(1, reach_blocks + 1)]
    )
    ordered = by_distance[::-1]
    missing = span_blocks - reach_blocks
    window_rows = (span_blocks + 1) * tok_rows
    key_window = ordered[:, 0].reshape(window_rows, kv_count, head_size)
    value_window = ordered[:, 1].reshape(window_rows, kv_count, head_size)
    doc_padded = jnp.concatenate([jnp.full((span_blocks,), -1, jnp.int32), block_doc])
    window_docs = lax.dynamic_slice_in_dim(doc_padded, own_block, span_blocks + 1, 0)
    key_docs = jnp.repeat(window_docs, tok_rows)
    own_doc = lax.dynamic_slice_in_dim(block_doc, own_block, 1, 0)
    rel_key = jnp.arange(window_rows, dtype=jnp.int32)
    rel_query = jnp.arange(tok_rows, dtype=jnp.int32) + span_blocks * tok_rows
    visible = (rel_key[None, :] <= rel_query[:, None]) & (
        rel_key[None, :] > rel_query[:, None] - WINDOW
    )
    visible = visible & (key_docs[None, :] == own_doc[0])
    query_heads = queries.reshape(tok_rows, kv_count, group_size, head_size)
    scores = (
        jnp.einsum("tkgd,skd->kgts", query_heads, key_window, preferred_element_type=jnp.float32)
        * query_scale
    )
    scores = jnp.where(visible[None, None], scores, -jnp.inf)
    top = jnp.max(scores, axis=-1, keepdims=True)
    expo = jnp.exp(scores - top)
    probs = expo / jnp.sum(expo, axis=-1, keepdims=True)
    probs_low = probs.astype(jnp.bfloat16)
    attn_heads = jnp.einsum(
        "kgts,skd->tkgd", probs_low, value_window, preferred_element_type=jnp.float32
    ).astype(jnp.bfloat16)
    attn = attn_heads.reshape(tok_rows, queries.shape[1])
    output_terms = jnp.dot(attn, out_weight, preferred_element_type=jnp.float32)
    attn_output = lax.psum_scatter(output_terms, "tp", scatter_dimension=1, tiled=True).astype(
        jnp.bfloat16
    )
    weight_terms = jnp.einsum("tr,tc->rc", attn, out_grad, preferred_element_type=jnp.float32)
    out_weight_grad = lax.psum_scatter(weight_terms, "ctx", scatter_dimension=1, tiled=True)
    d_attn = jnp.einsum(
        "te,re->tr", out_grad, out_weight, preferred_element_type=jnp.float32
    ).astype(jnp.bfloat16)
    d_attn_heads = d_attn.reshape(tok_rows, kv_count, group_size, head_size)
    d_probs = jnp.einsum(
        "tkgd,skd->kgts", d_attn_heads, value_window, preferred_element_type=jnp.float32
    )
    delta = jnp.einsum(
        "tkgd,tkgd->kgt", attn_heads, d_attn_heads, preferred_element_type=jnp.float32
    )
    d_scores = (probs * (d_probs - delta[..., None])).astype(jnp.bfloat16)
    query_grad = (
        jnp.einsum("kgts,skd->tkgd", d_scores, key_window, preferred_element_type=jnp.float32)
        * query_scale
    ).astype(jnp.bfloat16)
    query_grad = query_grad.reshape(tok_rows, queries.shape[1])
    key_part = (
        jnp.einsum("kgts,tkgd->skd", d_scores, query_heads, preferred_element_type=jnp.float32)
        * query_scale
    )
    value_part = jnp.einsum(
        "kgts,tkgd->skd", probs_low, d_attn_heads, preferred_element_type=jnp.float32
    )
    by_position = jnp.stack(
        [
            key_part.reshape(span_blocks + 1, tok_rows, key_width),
            value_part.reshape(span_blocks + 1, tok_rows, key_width),
        ],
        axis=1,
    )
    terms_near = by_position[::-1]
    total = terms_near[0] + sum(
        [shifted(terms_near[distance], "ctx", -distance) for distance in range(1, reach_blocks + 1)]
    )
    key_grad = total[0].astype(jnp.bfloat16)
    value_grad = total[1].astype(jnp.bfloat16)
    return (attn_output, query_grad, key_grad, value_grad, out_weight_grad)


def solution(mesh):
    placed = (P("ctx", "tp"), P("ctx", "tp"), P("ctx", "tp"), P("tp", None), P("ctx", None), P())
    return jax.shard_map(
        local,
        mesh=mesh,
        in_specs=placed,
        out_specs=(P("ctx", "tp"), P("ctx", "tp"), P("ctx", "tp"), P("ctx", "tp"), P("tp", "ctx")),
        check_vma=False,
    )
```

profile of v0, /device:TPU:22, one launch (start us, length us, event | category | flops | bytes accessed | tf_op | source)
XLA Modules:
  0.0 250.0 jit_solution(18397767400417977334)
XLA Ops:
  7.2 1.0 pad_maximum_fusion.1
  8.2 10.6 %collective-permute-start.2 = (bf16[2,256,128]{2,1,0:T(8,128)(2,1)S(1)}, bf16[2,256,128]{2,1,0:T(8,128)(2,1)S(1)}, u32[]{:S(2)}, u32[]{:S(2)}) collective-permute-start(bf16[2,256,128]{2,1,0:T(8,128)(2,1)S(1)} %pad_maximum_fusion.1), channel_id=1, source_target_pairs={{0,48},{16,64},{32,80},{48,96},{64,112},{80,128},{96,144},{112,160... | collective-permute-start | bytes 393224 | tf_op jit(solution)/shard_map/ppermute | solution.py:16
  18.8 8.2 %collective-permute-start.1 = (bf16[2,256,128]{2,1,0:T(8,128)(2,1)S(1)}, bf16[2,256,128]{2,1,0:T(8,128)(2,1)S(1)}, u32[]{:S(2)}, u32[]{:S(2)}) collective-permute-start(bf16[2,256,128]{2,1,0:T(8,128)(2,1)S(1)} %pad_maximum_fusion.1), channel_id=1, source_target_pairs={{0,32},{16,48},{32,64},{48,80},{64,96},{80,112},{96,128},{112,144}... | collective-permute-start | bytes 393224 | tf_op jit(solution)/shard_map/ppermute | solution.py:16
  27.1 4.3 %collective-permute-start = (bf16[2,256,128]{2,1,0:T(8,128)(2,1)S(1)}, bf16[2,256,128]{2,1,0:T(8,128)(2,1)S(1)}, u32[]{:S(2)}, u32[]{:S(2)}) collective-permute-start(bf16[2,256,128]{2,1,0:T(8,128)(2,1)S(1)} %pad_maximum_fusion.1), channel_id=1, source_target_pairs={{0,16},{16,32},{32,48},{48,64},{64,80},{80,96},{96,112},{112,128},... | collective-permute-start | bytes 393224 | tf_op jit(solution)/shard_map/ppermute | solution.py:16
  31.4 3.7 %collective-permute-start.3 = (bf16[2,256,128]{2,1,0:T(8,128)(2,1)S(1)}, bf16[2,256,128]{2,1,0:T(8,128)(2,1)S(1)}, u32[]{:S(2)}, u32[]{:S(2)}) collective-permute-start(bf16[2,256,128]{2,1,0:T(8,128)(2,1)S(1)} %pad_maximum_fusion.1), channel_id=1, source_target_pairs={{0,64},{16,80},{32,96},{48,112},{64,128},{80,144},{96,160},{112,17... | collective-permute-start | bytes 393224 | tf_op jit(solution)/shard_map/ppermute | solution.py:16
  35.1 1.2 dynamic_slice.7
  36.4 1.4 dynamic-slice_compare_fusion
  38.2 1.9 convolution_convert_fusion
  40.2 3.3 %collective-permute-done = bf16[2,256,128]{2,1,0:T(8,128)(2,1)S(1)} collective-permute-done((bf16[2,256,128]{2,1,0:T(8,128)(2,1)S(1)}, bf16[2,256,128]{2,1,0:T(8,128)(2,1)S(1)}, u32[]{:S(2)}, u32[]{:S(2)}) %collective-permute-start) | collective-permute-done | bytes 131104 | tf_op jit(solution)/shard_map/ppermute | solution.py:16
  43.6 3.2 %collective-permute-done.3 = bf16[2,256,128]{2,1,0:T(8,128)(2,1)S(1)} collective-permute-done((bf16[2,256,128]{2,1,0:T(8,128)(2,1)S(1)}, bf16[2,256,128]{2,1,0:T(8,128)(2,1)S(1)}, u32[]{:S(2)}, u32[]{:S(2)}) %collective-permute-start.3) | collective-permute-done | bytes 131104 | tf_op jit(solution)/shard_map/ppermute | solution.py:16
  47.0 0.8 copy-done.10
  47.7 0.5 fusion.37
  48.3 0.4 fusion.9
  48.6 0.4 fusion.19
  49.1 0.7 copy-done.1
  49.8 0.4 fusion.31
  50.2 2.2 fusion.38
  52.4 1.3 dynamic-slice.4
  54.3 3.6 %fusion.39 = f32[256,2688]{0,1:T(8,128)} fusion(bf16[256,256]{0,1:T(8,128)(2,1)S(1)} %bitcast.152, bf16[256,2688]{1,0:T(8,128)(2,1)} %param.10), kind=kOutput, calls=%fused_computation.66 | convolution fusion | flops 352321536 | bytes 4259840 | tf_op jit(solution)/shard_map/tr,tc->rc/dot_general | solution.py:65
  57.9 88.8 %fusion = f32[256,48]{0,1:T(8,128)S(1)} fusion(f32[256,2688]{0,1:T(8,128)} %fusion.39), kind=kCustom, calls=%all-reduce-scatter | all-reduce-scatter fusion | flops 786433 | bytes 2805760
  146.7 0.6 slice.63
  147.3 1.9 collective-permute-start.14
  149.2 4.8 %collective-permute-start.13 = (f32[256,48]{0,1:T(8,128)S(1)}, f32[256,48]{0,1:T(8,128)}, u32[]{:S(2)}, u32[]{:S(2)}) collective-permute-start(f32[256,48]{0,1:T(8,128)S(1)} %fusion), channel_id=1, source_target_pairs={{0,96},{16,112},{32,128},{48,144},{64,160},{80,176},{96,192},{112,... | collective-permute-start | bytes 147464
  154.0 4.3 %collective-permute-start.12 = (f32[256,48]{0,1:T(8,128)S(1)}, f32[256,48]{0,1:T(8,128)}, u32[]{:S(2)}, u32[]{:S(2)}) collective-permute-start(f32[256,48]{0,1:T(8,128)S(1)} %fusion), channel_id=1, source_target_pairs={{0,80},{16,96},{32,112},{48,128},{64,144},{80,160},{96,176},{112,1... | collective-permute-start | bytes 147464
  158.4 5.6 %collective-permute-start.11 = (f32[256,48]{0,1:T(8,128)S(1)}, f32[256,48]{0,1:T(8,128)}, u32[]{:S(2)}, u32[]{:S(2)}) collective-permute-start(f32[256,48]{0,1:T(8,128)S(1)} %fusion), channel_id=1, source_target_pairs={{0,64},{16,80},{32,96},{48,112},{64,128},{80,144},{96,160},{112,17... | collective-permute-start | bytes 147464
  164.0 2.0 collective-permute-start.15
  166.0 0.5 convolution_bitcast_fusion.1
  166.5 2.4 fusion.6
  169.0 1.1 copy-done.2
  170.1 0.5 fusion.7
  170.8 4.1 %collective-permute-start.10 = (f32[256,48]{0,1:T(8,128)S(1)}, f32[256,48]{0,1:T(8,128)S(1)}, u32[]{:S(2)}, u32[]{:S(2)}) collective-permute-start(f32[256,48]{0,1:T(8,128)S(1)} %fusion), channel_id=1, source_target_pairs={{0,48},{16,64},{32,80},{48,96},{64,112},{80,128},{96,144},{112,160... | collective-permute-start | bytes 147464
  174.9 3.4 %collective-permute-start.9 = (f32[256,48]{0,1:T(8,128)S(1)}, f32[256,48]{0,1:T(8,128)S(1)}, u32[]{:S(2)}, u32[]{:S(2)}) collective-permute-start(f32[256,48]{0,1:T(8,128)S(1)} %fusion), channel_id=1, source_target_pairs={{0,32},{16,48},{32,64},{48,80},{64,96},{80,112},{96,128},{112,144}... | collective-permute-start | bytes 147464
  178.4 0.9 fusion.29
  179.3 2.4 collective-permute-start.8
  181.8 6.7 %collective-permute-start.5 = (f32[2,256,128]{2,1,0:T(8,128)}, f32[2,256,128]{2,1,0:T(8,128)}, u32[]{:S(2)}, u32[]{:S(2)}) collective-permute-start(f32[2,256,128]{2,1,0:T(8,128)} %get-tuple-element.20), channel_id=1, source_target_pairs={{32,0},{48,16},{64,32},{80,48},{96,64},{112,80},{128,96},{144,112}... | collective-permute-start | bytes 786440 | tf_op jit(solution)/shard_map/ppermute | solution.py:16
  188.5 2.1 collective-permute-start.4
  190.6 4.6 %collective-permute-start.7 = (f32[2,256,128]{2,1,0:T(8,128)}, f32[2,256,128]{2,1,0:T(8,128)}, u32[]{:S(2)}, u32[]{:S(2)}) collective-permute-start(f32[2,256,128]{2,1,0:T(8,128)} %get-tuple-element.22), channel_id=1, source_target_pairs={{64,0},{80,16},{96,32},{112,48},{128,64},{144,80},{160,96},{176,11... | collective-permute-start | bytes 786440 | tf_op jit(solution)/shard_map/ppermute | solution.py:16
  195.3 0.6 copy-done.12
  195.9 5.5 %collective-permute-start.6 = (f32[2,256,128]{2,1,0:T(8,128)S(1)}, f32[2,256,128]{2,1,0:T(8,128)}, u32[]{:S(2)}, u32[]{:S(2)}) collective-permute-start(f32[2,256,128]{2,1,0:T(8,128)S(1)} %get-tuple-element.23), channel_id=1, source_target_pairs={{48,0},{64,16},{80,32},{96,48},{112,64},{128,80},{144,96},{160,112... | collective-permute-start | bytes 786440 | tf_op jit(solution)/shard_map/ppermute | solution.py:16
  201.5 0.4 fusion.15
  201.8 0.8 copy.49
  202.6 6.2 %concatenate.4 = f32[256,426]{0,1:T(8,128)S(1)} concatenate(f32[256,42]{0,1:T(8,128)} %collective-permute-done.15, f32[256,48]{0,1:T(8,128)} %collective-permute-done.14, f32[256,48]{0,1:T(8,128)} %collective-permute-done.13, f32[256,48]{0,1:T(8,128)} %collective-permute-done.12, f32[256,48]{0,1:T(8,128)} %collective-permute-done.11, f32[256,48]{0,1:T(8,128)S(1)} %collective-permute-done.10, ...), dimensions={1} | concatenate | bytes 872448
  208.8 0.6 constant_dynamic-slice_fusion
  209.5 24.7 %collective-permute-done.5 = f32[2,256,128]{2,1,0:T(8,128)} collective-permute-done((f32[2,256,128]{2,1,0:T(8,128)}, f32[2,256,128]{2,1,0:T(8,128)}, u32[]{:S(2)}, u32[]{:S(2)}) %collective-permute-start.5) | collective-permute-done | bytes 262176 | tf_op jit(solution)/shard_map/ppermute | solution.py:16
  234.1 5.6 %collective-permute-done.6 = f32[2,256,128]{2,1,0:T(8,128)} collective-permute-done((f32[2,256,128]{2,1,0:T(8,128)S(1)}, f32[2,256,128]{2,1,0:T(8,128)}, u32[]{:S(2)}, u32[]{:S(2)}) %collective-permute-start.6) | collective-permute-done | bytes 262176 | tf_op jit(solution)/shard_map/ppermute | solution.py:16
  239.7 1.3 fusion.25
  240.9 0.7 slice_bitcast_fusion
  241.6 1.6 convert_element_type.42
  (50 shorter events, 1.0 us)
Async XLA Ops:
  7.2 31.0 %copy-start = (bf16[256,2688]{1,0:T(8,128)(2,1)S(1)}, bf16[256,2688]{1,0:T(8,128)(2,1)}, u32[]{:S(2)}) copy-start(bf16[256,2688]{1,0:T(8,128)(2,1)} %param.9) | copy-start | bytes 4128772
  7.2 234.4 %reduce-scatter.4.cloned.1.call-start = ((), (), s32[]{:S(2)}) async-start(), calls=%async_computation.1 | async-start | bytes 2924544 | tf_op jit(solution)/shard_map/reduce_scatter | solution.py:62
  8.2 35.4 %collective-permute-start.2 = (bf16[2,256,128]{2,1,0:T(8,128)(2,1)S(1)}, bf16[2,256,128]{2,1,0:T(8,128)(2,1)S(1)}, u32[]{:S(2)}, u32[]{:S(2)}) collective-permute-start(bf16[2,256,128]{2,1,0:T(8,128)(2,1)S(1)} %pad_maximum_fusion.1), channel_id=1, source_target_pairs={{0,48},{16,64},{32,80},{48,96},{64,112},{80,128},{96,144},{112,160... | collective-permute-start | bytes 393224 | tf_op jit(solution)/shard_map/ppermute | solution.py:16
  18.8 24.7 %collective-permute-start.1 = (bf16[2,256,128]{2,1,0:T(8,128)(2,1)S(1)}, bf16[2,256,128]{2,1,0:T(8,128)(2,1)S(1)}, u32[]{:S(2)}, u32[]{:S(2)}) collective-permute-start(bf16[2,256,128]{2,1,0:T(8,128)(2,1)S(1)} %pad_maximum_fusion.1), channel_id=1, source_target_pairs={{0,32},{16,48},{32,64},{48,80},{64,96},{80,112},{96,128},{112,144}... | collective-permute-start | bytes 393224 | tf_op jit(solution)/shard_map/ppermute | solution.py:16
  27.1 16.5 %collective-permute-start = (bf16[2,256,128]{2,1,0:T(8,128)(2,1)S(1)}, bf16[2,256,128]{2,1,0:T(8,128)(2,1)S(1)}, u32[]{:S(2)}, u32[]{:S(2)}) collective-permute-start(bf16[2,256,128]{2,1,0:T(8,128)(2,1)S(1)} %pad_maximum_fusion.1), channel_id=1, source_target_pairs={{0,16},{16,32},{32,48},{48,64},{64,80},{80,96},{96,112},{112,128},... | collective-permute-start | bytes 393224 | tf_op jit(solution)/shard_map/ppermute | solution.py:16
  31.4 15.4 %collective-permute-start.3 = (bf16[2,256,128]{2,1,0:T(8,128)(2,1)S(1)}, bf16[2,256,128]{2,1,0:T(8,128)(2,1)S(1)}, u32[]{:S(2)}, u32[]{:S(2)}) collective-permute-start(bf16[2,256,128]{2,1,0:T(8,128)(2,1)S(1)} %pad_maximum_fusion.1), channel_id=1, source_target_pairs={{0,64},{16,80},{32,96},{48,112},{64,128},{80,144},{96,160},{112,17... | collective-permute-start | bytes 393224 | tf_op jit(solution)/shard_map/ppermute | solution.py:16
  38.2 2.0 copy-start.8
  38.2 2.0 copy-start.9
  46.8 0.9 copy-start.10
  46.9 1.3 copy-start.4
  47.0 2.8 %copy-start.6 = (bf16[5,1,256,128]{3,2,1,0:T(8,128)(2,1)}, bf16[5,1,256,128]{3,2,1,0:T(8,128)(2,1)S(1)}, u32[]{:S(2)}) copy-start(bf16[5,1,256,128]{3,2,1,0:T(8,128)(2,1)S(1)} %slice.41) | copy-start | bytes 983044
  48.3 1.5 copy-start.1
  146.7 19.8 %copy-start.7 = (bf16[5,1,256,128]{3,2,1,0:T(8,128)(2,1)S(1)}, bf16[5,1,256,128]{3,2,1,0:T(8,128)(2,1)}, u32[]{:S(2)}) copy-start(bf16[5,1,256,128]{3,2,1,0:T(8,128)(2,1)} %copy-done.6) | copy-start | bytes 983044
  147.3 27.6 %collective-permute-start.14 = (f32[256,48]{0,1:T(8,128)S(1)}, f32[256,48]{0,1:T(8,128)}, u32[]{:S(2)}, u32[]{:S(2)}) collective-permute-start(f32[256,48]{0,1:T(8,128)S(1)} %fusion), channel_id=1, source_target_pairs={{0,112},{16,128},{32,144},{48,160},{64,176},{80,192},{96,208},{112... | collective-permute-start | bytes 147464
  149.2 30.1 %collective-permute-start.13 = (f32[256,48]{0,1:T(8,128)S(1)}, f32[256,48]{0,1:T(8,128)}, u32[]{:S(2)}, u32[]{:S(2)}) collective-permute-start(f32[256,48]{0,1:T(8,128)S(1)} %fusion), channel_id=1, source_target_pairs={{0,96},{16,112},{32,128},{48,144},{64,160},{80,176},{96,192},{112,... | collective-permute-start | bytes 147464
  154.0 27.7 %collective-permute-start.12 = (f32[256,48]{0,1:T(8,128)S(1)}, f32[256,48]{0,1:T(8,128)}, u32[]{:S(2)}, u32[]{:S(2)}) collective-permute-start(f32[256,48]{0,1:T(8,128)S(1)} %fusion), channel_id=1, source_target_pairs={{0,80},{16,96},{32,112},{48,128},{64,144},{80,160},{96,176},{112,1... | collective-permute-start | bytes 147464
  158.4 30.1 %collective-permute-start.11 = (f32[256,48]{0,1:T(8,128)S(1)}, f32[256,48]{0,1:T(8,128)}, u32[]{:S(2)}, u32[]{:S(2)}) collective-permute-start(f32[256,48]{0,1:T(8,128)S(1)} %fusion), channel_id=1, source_target_pairs={{0,64},{16,80},{32,96},{48,112},{64,128},{80,144},{96,160},{112,17... | collective-permute-start | bytes 147464
  164.0 6.8 %collective-permute-start.15 = (f32[256,42]{0,1:T(8,128)}, f32[256,42]{0,1:T(8,128)}, u32[]{:S(2)}, u32[]{:S(2)}) collective-permute-start(f32[256,42]{0,1:T(8,128)} %slice.63), channel_id=1, source_target_pairs={{0,128},{16,144},{32,160},{48,176},{64,192},{80,208},{96,224},{112... | collective-permute-start | bytes 129032
  166.5 3.5 %copy-start.11 = (bf16[256,256]{1,0:T(8,128)(2,1)S(1)}, bf16[256,256]{1,0:T(8,128)(2,1)}, u32[]{:S(2)}) copy-start(bf16[256,256]{1,0:T(8,128)(2,1)} %param.6) | copy-start | bytes 393220
  169.0 1.1 copy-start.2
  170.8 30.6 %copy-start.3 = (bf16[2,256,1280]{1,2,0:T(8,128)(2,1)S(1)}, bf16[2,256,1280]{1,2,0:T(8,128)(2,1)}, u32[]{:S(2)}) copy-start(bf16[2,256,1280]{1,2,0:T(8,128)(2,1)} %copy-done.2) | copy-start | bytes 3932164
  170.8 30.6 %copy-start.5 = (bf16[5,1,256,128]{3,2,1,0:T(8,128)(2,1)S(1)}, bf16[5,1,256,128]{3,2,1,0:T(8,128)(2,1)}, u32[]{:S(2)}) copy-start(bf16[5,1,256,128]{3,2,1,0:T(8,128)(2,1)} %copy-done.4) | copy-start | bytes 983044
  170.8 19.8 %collective-permute-start.10 = (f32[256,48]{0,1:T(8,128)S(1)}, f32[256,48]{0,1:T(8,128)S(1)}, u32[]{:S(2)}, u32[]{:S(2)}) collective-permute-start(f32[256,48]{0,1:T(8,128)S(1)} %fusion), channel_id=1, source_target_pairs={{0,48},{16,64},{32,80},{48,96},{64,112},{80,128},{96,144},{112,160... | collective-permute-start | bytes 147464
  174.9 20.3 %collective-permute-start.9 = (f32[256,48]{0,1:T(8,128)S(1)}, f32[256,48]{0,1:T(8,128)S(1)}, u32[]{:S(2)}, u32[]{:S(2)}) collective-permute-start(f32[256,48]{0,1:T(8,128)S(1)} %fusion), channel_id=1, source_target_pairs={{0,32},{16,48},{32,64},{48,80},{64,96},{80,112},{96,128},{112,144}... | collective-permute-start | bytes 147464
  179.3 23.3 %collective-permute-start.8 = (f32[256,48]{0,1:T(8,128)S(1)}, f32[256,48]{0,1:T(8,128)}, u32[]{:S(2)}, u32[]{:S(2)}) collective-permute-start(f32[256,48]{0,1:T(8,128)S(1)} %fusion), channel_id=1, source_target_pairs={{0,16},{16,32},{32,48},{48,64},{64,80},{80,96},{96,112},{112,128},... | collective-permute-start | bytes 147464
  181.8 52.4 %collective-permute-start.5 = (f32[2,256,128]{2,1,0:T(8,128)}, f32[2,256,128]{2,1,0:T(8,128)}, u32[]{:S(2)}, u32[]{:S(2)}) collective-permute-start(f32[2,256,128]{2,1,0:T(8,128)} %get-tuple-element.20), channel_id=1, source_target_pairs={{32,0},{48,16},{64,32},{80,48},{96,64},{112,80},{128,96},{144,112}... | collective-permute-start | bytes 786440 | tf_op jit(solution)/shard_map/ppermute | solution.py:16
  188.5 45.7 %collective-permute-start.4 = (f32[2,256,128]{2,1,0:T(8,128)}, f32[2,256,128]{2,1,0:T(8,128)}, u32[]{:S(2)}, u32[]{:S(2)}) collective-permute-start(f32[2,256,128]{2,1,0:T(8,128)} %get-tuple-element.21), channel_id=1, source_target_pairs={{16,0},{32,16},{48,32},{64,48},{80,64},{96,80},{112,96},{128,112},... | collective-permute-start | bytes 786440 | tf_op jit(solution)/shard_map/ppermute | solution.py:16
  190.6 43.5 %collective-permute-start.7 = (f32[2,256,128]{2,1,0:T(8,128)}, f32[2,256,128]{2,1,0:T(8,128)}, u32[]{:S(2)}, u32[]{:S(2)}) collective-permute-start(f32[2,256,128]{2,1,0:T(8,128)} %get-tuple-element.22), channel_id=1, source_target_pairs={{64,0},{80,16},{96,32},{112,48},{128,64},{144,80},{160,96},{176,11... | collective-permute-start | bytes 786440 | tf_op jit(solution)/shard_map/ppermute | solution.py:16
  195.3 0.6 copy-start.12
  195.9 43.8 %collective-permute-start.6 = (f32[2,256,128]{2,1,0:T(8,128)S(1)}, f32[2,256,128]{2,1,0:T(8,128)}, u32[]{:S(2)}, u32[]{:S(2)}) collective-permute-start(f32[2,256,128]{2,1,0:T(8,128)S(1)} %get-tuple-element.23), channel_id=1, source_target_pairs={{48,0},{64,16},{80,32},{96,48},{112,64},{128,80},{144,96},{160,112... | collective-permute-start | bytes 786440 | tf_op jit(solution)/shard_map/ppermute | solution.py:16
Sparse Core Ops, SparseCore 0:
  52.5 64.9 reduce-scatter.3
where the time goes:
time: 251 us; the launch traced here: 250 us
  blocking collectives  88.8 us (35%)
  starting transfers between devices  74.5 us (30%)
  waiting for transfers between devices  36.8 us (15%)
  between operations  15.2 us (6%)
  local copies, waits for them, and re-layouts  15.1 us (6%)
  matrix products  12.5 us (5%)
  other arithmetic  7.23 us (3%)
    unnamed x1, blocking collectives  88.8 us
    ppermute x8, starting transfers between devices, shifted(): return lax.ppermute(shard, axis, pairs)  45.9 us
    ppermute x8, waiting for transfers between devices, shifted(): return lax.ppermute(shard, axis, pairs)  36.7 us
    unnamed x8, starting transfers between devices  28.6 us
    unnamed x34, local copies, waits for them, and re-layouts  12.8 us
  transfers between devices with their start and end apart: 17, of which 4 were waited for; matrix products, arithmetic and copies ran while one was open for 46% of the time, Pallas kernels for 0%

commit v1 on v0

v1 whole, which is shorter than its diff:
```python
import functools
import math

import jax
import jax.numpy as jnp
from jax import lax
from jax.experimental import pallas as pl
from jax.experimental.pallas import tpu as pltpu
from jax.sharding import PartitionSpec as P

MESH = pl.DeviceIdType.MESH
HEAD = 128
HEADS = 2
REACH = 4
query_scale = 168.0 ** -0.5
EXPONENT = query_scale * math.log2(math.e)
HIDDEN = -1e30
F32, BF16 = jnp.float32, jnp.bfloat16


def dot(a, b, a_dim, b_dim):
    return lax.dot_general(a, b, (((a_dim,), (b_dim,)), ((), ())), preferred_element_type=F32)


def ring_slots(n):
    length = {}
    for half in (0, 1):
        far, near = n // 2, n - 1 - n // 2
        length[half, 1] = far if half == 0 else near
        length[half, -1] = near if half == 0 else far
    slot = {}
    for key, steps in length.items():
        for step in range(1, steps + 1):
            slot[key + (step,)] = len(slot)
    return slot, length


def kernel(nx, ny, nz, doc, q_in, k_in, v_in, w_in, g_in, out_o, dq_o, dk_o, dv_o, dw_o, *scratch):
    (q_s, k_s, v_s, w_s, g_s, wt_s, gt_s, p_s, dp_s, at_s, do_s, dot_s, xs, xr, ys, yr, gs, gr,
     za, zf, zs, zr, ya, cs, cr,
     load_sem, k_snd, k_rcv, v_snd, v_rcv, x_snd, x_rcv, y_snd, y_rcv, g_snd, g_rcv, z_snd, z_rcv, c_snd, c_rcv) = scratch
    n_ctx = nx * nz
    ctx, tp = lax.axis_index("ctx"), lax.axis_index("tp")
    x, z = ctx // nz, ctx % nz
    y, core = tp // 2, tp % 2
    following, preceding = ((ctx + 1) % n_ctx, tp), ((ctx + n_ctx - 1) % n_ctx, tp)
    x_next = {1: ((x + 1) % nx * nz + z, tp), -1: ((x + nx - 1) % nx * nz + z, tp)}
    y_next = {1: (ctx, (y + 1) % ny * 2 + core), -1: (ctx, (y + ny - 1) % ny * 2 + core)}
    partner = (ctx, y * 2 + 1 - core)
    z_peer = {o: (x * nz + (z + o) % nz, tp) for o in range(1, nz)}
    chunk_x, chunk_y = gt_s.shape[0] // nx, wt_s.shape[0] // ny
    piece = chunk_x // nz

    loads = [pltpu.make_async_copy(src, dst, load_sem.at[i]) for i, (src, dst) in enumerate(
        [(k_in, k_s.at[0]), (q_in, q_s), (v_in, v_s.at[0]), (g_in, g_s), (w_in, w_s)])]
    for load in loads:
        load.start()
    barrier = pltpu.get_barrier_semaphore()
    greeted = [following, preceding, *x_next.values(), *y_next.values(), partner, *z_peer.values()]
    for device in greeted:
        pl.semaphore_signal(barrier, inc=1, device_id=device, device_id_type=MESH)
    pl.semaphore_wait(barrier, len(greeted))

    def send(src, dst, snd, rcv, device):
        copy = pltpu.make_async_remote_copy(src_ref=src, dst_ref=dst, send_sem=snd, recv_sem=rcv, device_id=device,
                                            device_id_type=MESH)
        copy.start()
        return copy

    k_copy, v_copy = {}, {}

    def pass_k(d):
        k_copy[d] = send(k_in if d == 0 else k_s.at[d], k_s.at[d + 1], k_snd.at[d], k_rcv.at[d], following)

    def pass_v(d):
        v_copy[d] = send(v_in if d == 0 else v_s.at[d], v_s.at[d + 1], v_snd.at[d], v_rcv.at[d], following)

    pass_k(0)
    pass_v(0)

    own_doc = doc[ctx]
    bias = [None] + [
        jnp.where((ctx >= d) & (doc[(ctx + n_ctx - d) % n_ctx] == own_doc), 0.0, HIDDEN).astype(F32)
        for d in range(1, REACH + 1)
    ]
    size = q_s.shape[0]
    key_at = lax.broadcasted_iota(jnp.int32, (size, size), 0)
    query_at = lax.broadcasted_iota(jnp.int32, (size, size), 1)

    def head(ref, h):
        return ref[:, h * HEAD:(h + 1) * HEAD]

    top, top_at, total, acc = {}, {}, {}, {}

    def attend(d):
        for h in range(HEADS):
            s = dot(k_s[d], head(q_s, h), 1, 1)
            if d == 0:
                s = jnp.where(key_at <= query_at, s, HIDDEN)
            if d == REACH:
                s = jnp.where(key_at > query_at, s, HIDDEN)
            most = jnp.max(s, axis=0, keepdims=True) * EXPONENT
            if d > 0:
                most = jnp.maximum(top[h], most + bias[d])
            p = jnp.exp2(s * EXPONENT - (most if d == 0 else most - bias[d]))
            p_s[d, h] = p
            rows = jnp.sum(p, axis=0, keepdims=True)
            if d == 0:
                total[h] = rows
            else:
                fade = jnp.exp2(top[h] - most)
                total[h] = total[h] * fade + rows
                acc[h] = acc[h] * fade
            top[h] = top_at[d, h] = most

    def weigh(d):
        for h in range(HEADS):
            part = dot(v_s[d], p_s[d, h].astype(BF16), 0, 0)
            acc[h] = part if d == 0 else acc[h] + part

    def value_side(d):
        for h in range(HEADS):
            dp_s[d, h] = dot(v_s[d], head(do_s, h), 1, 1)

    def turn(src, dst):
        for j in range(src.shape[1] // 128):
            dst[j * 128:(j + 1) * 128, :] = src[:, j * 128:(j + 1) * 128].T

    for load in loads[:3]:
        load.wait()
    attend(0)
    weigh(0)
    for load in loads[3:]:
        load.wait()
    do_s[...] = dot(g_s[...], w_s[...], 1, 1).astype(BF16)
    for d in range(1, REACH + 1):
        k_copy[d - 1].wait_recv()
        if d < REACH:
            pass_k(d)
        if d > 1:
            attend(d)
        v_copy[d - 1].wait_recv()
        if d < REACH:
            pass_v(d)
        if d == 1:
            attend(d)
            dot_s[...] = dot(w_s[...], g_s[...], 1, 1).astype(BF16)
        weigh(d)
        if d == 1:
            value_side(0)
            value_side(1)
        elif d < REACH:
            value_side(d)
        if d == 2:
            turn(g_s, gt_s)
        if d == 3:
            turn(w_s, wt_s)

    share, delta = {}, {}
    for h in range(HEADS):
        share[h] = 1.0 / total[h]
        attn = (acc[h] * share[h]).astype(BF16)
        at_s[h * HEAD:(h + 1) * HEAD, :] = attn
        delta[h] = jnp.sum(attn.astype(F32) * dot_s[h * HEAD:(h + 1) * HEAD, :].astype(F32), axis=0, keepdims=True)

    def weight_term(at, half):
        rows = gt_s[pl.ds(pl.multiple_of(at * chunk_x, 16), chunk_x), :]
        return dot(rows, at_s[half * 128:(half + 1) * 128, :], 1, 1)

    def output_term(at, half):
        rows = wt_s[pl.ds(pl.multiple_of(at * chunk_y, 16), chunk_y), :]
        return dot(rows, at_s[:, half * 128:(half + 1) * 128], 1, 0)

    x_slot, x_len = ring_slots(nx)
    y_slot, y_len = ring_slots(ny)
    chains = {"x": (weight_term, x, nx, x_next, xs, xr, x_snd, x_rcv, x_slot, x_len, {}),
              "y": (output_term, y, ny, y_next, ys, yr, y_snd, y_rcv, y_slot, y_len, {})}

    def chain_step(name, step):
        term, me, n, neighbour, out, arrived, snd, rcv, slot, length, copies = chains[name]
        for half in (0, 1):
            for way in (1, -1):
                if step > length[half, way]:
                    continue
                at = (me + n + way * (length[half, way] - step + 1)) % n
                part = term(at, half)
                if step > 1:
                    before = half, way, step - 1
                    copies[before].wait_recv()
                    part = part + arrived[slot[before]].astype(F32)
                now = slot[half, way, step]
                out[now] = part.astype(BF16)
                copies[half, way, step] = send(out.at[now], arrived.at[now], snd.at[now], rcv.at[now], neighbour[way])

    def chain_end(name, half):
        term, me, n, neighbour, out, arrived, snd, rcv, slot, length, copies = chains[name]
        part = term(me, half)
        for way in (1, -1):
            steps = length[half, way]
            if steps:
                copies[half, way, steps].wait_recv()
                part = part + arrived[slot[half, way, steps]].astype(F32)
        return part

    query_part, grad_copies = {}, {}

    def backward(d):
        key_part = value_part = None
        for h in range(HEADS):
            probs = p_s[d, h] * (jnp.exp2(top_at[d, h] - top[h]) * share[h])
            d_scores = (probs * (dp_s[d, h] - delta[h])).astype(BF16)
            to_value = dot(probs.astype(BF16), head(do_s, h), 1, 0)
            to_key = dot(d_scores, head(q_s, h), 1, 0)
            to_query = dot(k_s[d], d_scores, 0, 0)
            query_part[h] = query_part[h] + to_query if h in query_part else to_query
            key_part = to_key if key_part is None else key_part + to_key
            value_part = to_value if value_part is None else value_part + to_value
        return key_part, value_part

    def grad_step(step):
        parts = backward(REACH + 1 - step)
        for kind in (0, 1):
            part = parts[kind]
            if step > 1:
                grad_copies[step - 1, kind].wait_recv()
                part = part + gr[step - 2, kind].astype(F32)
            gs[step - 1, kind] = part.astype(BF16)
            grad_copies[step, kind] = send(gs.at[step - 1, kind], gr.at[step - 1, kind], g_snd.at[step - 1, kind],
                                           g_rcv.at[step - 1, kind], preceding)

    steps_x, steps_y = max(x_len.values()), max(y_len.values())
    for step in range(1, max(steps_x, steps_y, REACH) + 1):
        if step <= steps_x:
            chain_step("x", step)
        if step <= steps_y:
            chain_step("y", step)
        if step == 1:
            value_side(REACH)
        if step <= REACH:
            grad_step(step)

    z_copies = {}
    for half in (0, 1):
        za[0:chunk_x, :] = chain_end("x", half)
        za[chunk_x:, :] = jnp.zeros((za.shape[0] - chunk_x, 128), F32)
        for i in range(nz):
            rows = za[i * piece:i * piece + zf.shape[2], :]
            zf[half, i] = rows
            zs[half, i] = rows.astype(BF16)
        for o in sorted(range(1, nz), key=lambda o: -min(o, nz - o)):
            z_copies[half, o] = send(zs.at[half, (z + o) % nz], zr.at[half, o - 1], z_snd.at[half, o - 1],
                                     z_rcv.at[half, o - 1], z_peer[o])
    for half in (0, 1):
        ya[:, half * 128:(half + 1) * 128] = chain_end("y", half)
    mine = chunk_y // 2
    cs[...] = ya[pl.ds(pl.multiple_of((1 - core) * mine, 8), mine), :].astype(BF16)
    core_copy = send(cs, cr, c_snd, c_rcv, partner)

    key_part, value_part = backward(0)
    for h in range(HEADS):
        dq_o[h * HEAD:(h + 1) * HEAD, :] = (query_part[h] * query_scale).astype(BF16)
    grad_copies[REACH, 0].wait_recv()
    dk_o[...] = ((key_part + gr[REACH - 1, 0].astype(F32)) * query_scale).astype(BF16)
    grad_copies[REACH, 1].wait_recv()
    dv_o[...] = (value_part + gr[REACH - 1, 1].astype(F32)).astype(BF16)
    core_copy.wait_recv()
    out_o[...] = (ya[pl.ds(pl.multiple_of(core * mine, 8), mine), :] + cr[...].astype(F32)).astype(BF16)
    for half in (0, 1):
        part = zf[half, z]
        for o in range(1, nz):
            z_copies[half, o].wait_recv()
            part = part + zr[half, o - 1].astype(F32)
        dw_o[:, half * 128:(half + 1) * 128] = part
    for copies in (k_copy, v_copy, chains["x"][-1], chains["y"][-1], grad_copies, z_copies, {0: core_copy}):
        for copy in copies.values():
            copy.wait_send()


def local(nx, ny, nz, queries, keys, values, out_weight, out_grad, block_doc):
    size, width = queries.shape
    features = out_weight.shape[1]
    chunk_x, chunk_y = features // nx, features // ny
    piece = chunk_x // nz
    piece_rows = -(-piece // 16) * 16
    x_slots, y_slots = len(ring_slots(nx)[0]), len(ring_slots(ny)[0])
    DMA = pltpu.SemaphoreType.DMA
    V = pltpu.VMEM
    scratch = [
        V((size, width), BF16), V((REACH + 1, size, HEAD), BF16), V((REACH + 1, size, HEAD), BF16),
        V((width, features), BF16), V((size, features), BF16), V((features, width), BF16), V((features, size), BF16),
        V((REACH + 1, HEADS, size, size), F32), V((REACH + 1, HEADS, size, size), F32),
        V((width, size), BF16), V((size, width), BF16), V((width, size), BF16),
        V((x_slots, chunk_x, 128), BF16), V((x_slots, chunk_x, 128), BF16),
        V((y_slots, chunk_y, 128), BF16), V((y_slots, chunk_y, 128), BF16),
        V((REACH, 2, size, HEAD), BF16), V((REACH, 2, size, HEAD), BF16),
        V((chunk_x + piece_rows, 128), F32), V((2, nz, piece_rows, 128), F32), V((2, nz, piece_rows, 128), BF16),
        V((2, max(nz - 1, 1), piece_rows, 128), BF16),
        V((chunk_y, size), F32), V((chunk_y // 2, size), BF16), V((chunk_y // 2, size), BF16),
        DMA((5,)), DMA((REACH,)), DMA((REACH,)), DMA((REACH,)), DMA((REACH,)),
        DMA((x_slots,)), DMA((x_slots,)), DMA((y_slots,)), DMA((y_slots,)),
        DMA((REACH, 2)), DMA((REACH, 2)), DMA((2, nz - 1)), DMA((2, nz - 1)), DMA, DMA,
    ]
    anywhere, vmem = pl.BlockSpec(memory_space=pl.ANY), pl.BlockSpec(memory_space=pltpu.VMEM)
    out, dq, dk, dv, dw = pl.pallas_call(
        functools.partial(kernel, nx, ny, nz),
        out_shape=[
            jax.ShapeDtypeStruct((chunk_y // 2, size), BF16),
            jax.ShapeDtypeStruct((width, size), BF16),
            jax.ShapeDtypeStruct((size, HEAD), BF16),
            jax.ShapeDtypeStruct((size, HEAD), BF16),
            jax.ShapeDtypeStruct((piece_rows, width), F32),
        ],
        in_specs=[pl.BlockSpec(memory_space=pltpu.SMEM)] + [anywhere] * 5,
        out_specs=[vmem] * 5,
        scratch_shapes=scratch,
        compiler_params=pltpu.CompilerParams(collective_id=0, has_side_effects=True),
        name="layer",
    )(block_doc, queries, keys, values, out_weight, out_grad)
    return out.T, dq.T, dk, dv, dw[:piece].T


def solution(mesh, nx=8, ny=8, nz=8):
    placed = (P("ctx", "tp"), P("ctx", "tp"), P("ctx", "tp"), P("tp", None), P("ctx", None), P())
    return jax.shard_map(
        functools.partial(local, nx, ny, nz),
        mesh=mesh,
        in_specs=placed,
        out_specs=(P("ctx", "tp"), P("ctx", "tp"), P("ctx", "tp"), P("ctx", "tp"), P("tp", "ctx")),
        check_vma=False,
    )
```

time: 251 us -> 74.1 us (0.30)
  the two profiles are of different devices: /device:TPU:22 before, /device:TPU:14 now
where the time goes in v1:
time: 74.1 us; the launch traced here: 73.6 us
  Pallas kernels  65.4 us (88%)
  local copies, waits for them, and re-layouts  7.56 us (10%)
    pallas_call x1, Pallas kernels, local(): pl.pallas_call(functools.partial(kernel, nx, ny, nz), out_shape=[jax.Shap...  65.4 us
    unnamed x4, local copies, waits for them, and re-layouts  6.14 us

profile of v1, /device:TPU:14, one launch (start us, length us, event | category | flops | bytes accessed | tf_op | source)
XLA Modules:
  0.0 73.6 jit_solution(3389796480247554312)
XLA Ops:
  0.6 65.4 %layer.1 = (bf16[168,256]{1,0:T(8,128)(2,1)}, bf16[256,256]{1,0:T(8,128)(2,1)}, bf16[256,128]{1,0:T(8,128)(2,1)}, bf16[256,128]{1,0:T(8,128)(2,1)}, f32[48,256]{1,0:T(8,128)}) custom-call(s32[64]{0:T(128)} %doc.1, bf16[256,256]{1,0:T(8,128)(2,1)} %q_in.1, bf16[256,128]{1,0:T(8,128)(2,1)} %k_in.1, bf16[256,128]{1,0:T(8,128)(2,1)} %v_in.1, ...), custom_call_target="tpu_custom_call" | custom-call | tf_op jit(solution)/shard_map/layer/pallas_call | solution.py:304
  66.0 1.7 %copy.11 = bf16[256,256]{1,0:T(8,128)(2,1)} copy(bf16[256,256]{0,1:T(8,128)(2,1)} %bitcast.4) | data formatting | bytes 262144
  67.7 1.4 %slice_bitcast_fusion = f32[256,42]{0,1:T(8,128)} fusion(f32[48,256]{1,0:T(8,128)} %get-tuple-element.14), kind=kLoop, calls=%fused_computation | loop fusion | bytes 86016 | tf_op jit(solution)/shard_map/transpose | solution.py:319
  69.1 1.5 %copy.15 = bf16[256,168]{0,1:T(8,128)(2,1)} copy(bf16[256,168]{0,1:T(8,128)(2,1)} %bitcast.5) | data formatting | bytes 172032
  70.6 1.5 %copy.16 = bf16[256,128]{1,0:T(8,128)(2,1)} copy(bf16[256,128]{1,0:T(8,128)(2,1)} %get-tuple-element.27) | data formatting | bytes 131072
  72.1 1.5 %copy.17 = bf16[256,128]{1,0:T(8,128)(2,1)} copy(bf16[256,128]{1,0:T(8,128)(2,1)} %get-tuple-element.28) | data formatting | bytes 131072

commit v2 on v1

--- a/solution.py
+++ b/solution.py
@@ -37,8 +37,8 @@
 
 def kernel(nx, ny, nz, doc, q_in, k_in, v_in, w_in, g_in, out_o, dq_o, dk_o, dv_o, dw_o, *scratch):
     (q_s, k_s, v_s, w_s, g_s, wt_s, gt_s, p_s, dp_s, at_s, do_s, dot_s, xs, xr, ys, yr, gs, gr,
-     za, zf, zs, zr, ya, cs, cr,
-     load_sem, k_snd, k_rcv, v_snd, v_rcv, x_snd, x_rcv, y_snd, y_rcv, g_snd, g_rcv, z_snd, z_rcv, c_snd, c_rcv) = scratch
+     za, zf, zs, zr, ya, ls, lr, cs, cr,
+     load_sem, k_snd, k_rcv, v_snd, v_rcv, x_snd, x_rcv, y_snd, y_rcv, g_snd, g_rcv, z_snd, z_rcv, l_snd, l_rcv, c_snd, c_rcv) = scratch
     n_ctx = nx * nz
     ctx, tp = lax.axis_index("ctx"), lax.axis_index("tp")
     x, z = ctx // nz, ctx % nz
@@ -47,6 +47,7 @@
     x_next = {1: ((x + 1) % nx * nz + z, tp), -1: ((x + nx - 1) % nx * nz + z, tp)}
     y_next = {1: (ctx, (y + 1) % ny * 2 + core), -1: (ctx, (y + ny - 1) % ny * 2 + core)}
     partner = (ctx, y * 2 + 1 - core)
+    y_across = [(ctx, (y + way) % ny * 2 + 1 - core) for way in (1, ny - 1)]
     z_peer = {o: (x * nz + (z + o) % nz, tp) for o in range(1, nz)}
     chunk_x, chunk_y = gt_s.shape[0] // nx, wt_s.shape[0] // ny
     piece = chunk_x // nz
@@ -56,7 +57,7 @@
     for load in loads:
         load.start()
     barrier = pltpu.get_barrier_semaphore()
-    greeted = [following, preceding, *x_next.values(), *y_next.values(), partner, *z_peer.values()]
+    greeted = [following, preceding, *x_next.values(), *y_next.values(), *y_across, partner, *z_peer.values()]
     for device in greeted:
         pl.semaphore_signal(barrier, inc=1, device_id=device, device_id_type=MESH)
     pl.semaphore_wait(barrier, len(greeted))
@@ -76,7 +77,6 @@
         v_copy[d] = send(v_in if d == 0 else v_s.at[d], v_s.at[d + 1], v_snd.at[d], v_rcv.at[d], following)
 
     pass_k(0)
-    pass_v(0)
 
     own_doc = doc[ctx]
     bias = [None] + [
@@ -113,8 +113,8 @@
                 acc[h] = acc[h] * fade
             top[h] = top_at[d, h] = most
 
-    def weigh(d):
-        for h in range(HEADS):
+    def weigh(d, heads=range(HEADS)):
+        for h in heads:
             part = dot(v_s[d], p_s[d, h].astype(BF16), 0, 0)
             acc[h] = part if d == 0 else acc[h] + part
 
@@ -126,38 +126,37 @@
         for j in range(src.shape[1] // 128):
             dst[j * 128:(j + 1) * 128, :] = src[:, j * 128:(j + 1) * 128].T
 
-    for load in loads[:3]:
+    for load in loads[:2]:
         load.wait()
     attend(0)
+    k_copy[0].wait_send()
+    pass_v(0)
+    for load in loads[2:]:
+        load.wait()
     weigh(0)
-    for load in loads[3:]:
-        load.wait()
     do_s[...] = dot(g_s[...], w_s[...], 1, 1).astype(BF16)
     for d in range(1, REACH + 1):
         k_copy[d - 1].wait_recv()
         if d < REACH:
             pass_k(d)
-        if d > 1:
-            attend(d)
+        attend(d)
         v_copy[d - 1].wait_recv()
         if d < REACH:
             pass_v(d)
-        if d == 1:
-            attend(d)
-            dot_s[...] = dot(w_s[...], g_s[...], 1, 1).astype(BF16)
-        weigh(d)
-        if d == 1:
-            value_side(0)
-            value_side(1)
-        elif d < REACH:
+            weigh(d)
+            if d == 1:
+                dot_s[...] = dot(w_s[...], g_s[...], 1, 1).astype(BF16)
+                value_side(0)
             value_side(d)
-        if d == 2:
-            turn(g_s, gt_s)
-        if d == 3:
-            turn(w_s, wt_s)
+            if d == 2:
+                turn(g_s, gt_s)
+            if d == 3:
+                turn(w_s, wt_s)
 
     share, delta = {}, {}
-    for h in range(HEADS):
+
+    def conclude(h):
+        weigh(REACH, [h])
         share[h] = 1.0 / total[h]
         attn = (acc[h] * share[h]).astype(BF16)
         at_s[h * HEAD:(h + 1) * HEAD, :] = attn
@@ -176,24 +175,33 @@
     chains = {"x": (weight_term, x, nx, x_next, xs, xr, x_snd, x_rcv, x_slot, x_len, {}),
               "y": (output_term, y, ny, y_next, ys, yr, y_snd, y_rcv, y_slot, y_len, {})}
 
-    def chain_step(name, step):
+    last_copies = {}
+
+    def chain_step(name, half, step):
         term, me, n, neighbour, out, arrived, snd, rcv, slot, length, copies = chains[name]
-        for half in (0, 1):
-            for way in (1, -1):
-                if step > length[half, way]:
-                    continue
-                at = (me + n + way * (length[half, way] - step + 1)) % n
-                part = term(at, half)
-                if step > 1:
-                    before = half, way, step - 1
-                    copies[before].wait_recv()
-                    part = part + arrived[slot[before]].astype(F32)
-                now = slot[half, way, step]
-                out[now] = part.astype(BF16)
-                copies[half, way, step] = send(out.at[now], arrived.at[now], snd.at[now], rcv.at[now], neighbour[way])
-
-    def chain_end(name, half):
-        term, me, n, neighbour, out, arrived, snd, rcv, slot, length, copies = chains[name]
+        for way in (1, -1):
+            if step > length[half, way]:
+                continue
+            at = (me + n + way * (length[half, way] - step + 1)) % n
+            part = term(at, half)
+            if step > 1:
+                before = half, way, step - 1
+                copies[before].wait_recv()
+                part = part + arrived[slot[before]].astype(F32)
+            if name == "y" and step == length[half, way]:
+                side = (1 - way) // 2
+                for to in (0, 1):
+                    ls[half, side, to] = part[to * mine:(to + 1) * mine].astype(BF16)
+                    last_copies[half, side, to] = send(
+                        ls.at[half, side, to], lr.at[half, side, core], l_snd.at[half, side, to],
+                        l_rcv.at[half, side, core], (ctx, (y + ny + way) % ny * 2 + to))
+                continue
+            now = slot[half, way, step]
+            out[now] = part.astype(BF16)
+            copies[half, way, step] = send(out.at[now], arrived.at[now], snd.at[now], rcv.at[now], neighbour[way])
+
+    def weight_end(half):
+        term, me, n, neighbour, out, arrived, snd, rcv, slot, length, copies = chains["x"]
         part = term(me, half)
         for way in (1, -1):
             steps = length[half, way]
@@ -201,6 +209,19 @@
                 copies[half, way, steps].wait_recv()
                 part = part + arrived[slot[half, way, steps]].astype(F32)
         return part
+
+    def output_end(half):
+        columns = slice(half * 128, (half + 1) * 128)
+        part = ya[pl.ds(pl.multiple_of(core * mine, 8), mine), columns] + cr[:, columns].astype(F32)
+        for way in (1, -1):
+            if y_len[half, way]:
+                for source in (0, 1):
+                    side = (1 - way) // 2
+                    pltpu.make_async_remote_copy(
+                        src_ref=ls.at[half, side, 0], dst_ref=lr.at[half, side, source], send_sem=l_snd.at[half, side, 0],
+                        recv_sem=l_rcv.at[half, side, source], device_id=partner, device_id_type=MESH).wait_recv()
+                    part = part + lr[half, side, source].astype(F32)
+        out_o[:, columns] = part.astype(BF16)
 
     query_part, grad_copies = {}, {}
 
@@ -217,32 +238,49 @@
             value_part = to_value if value_part is None else value_part + to_value
         return key_part, value_part
 
-    def grad_step(step):
-        parts = backward(REACH + 1 - step)
-        for kind in (0, 1):
-            part = parts[kind]
-            if step > 1:
-                grad_copies[step - 1, kind].wait_recv()
-                part = part + gr[step - 2, kind].astype(F32)
-            gs[step - 1, kind] = part.astype(BF16)
-            grad_copies[step, kind] = send(gs.at[step - 1, kind], gr.at[step - 1, kind], g_snd.at[step - 1, kind],
-                                           g_rcv.at[step - 1, kind], preceding)
-
+    def grad_step(step, kind, part):
+        if step > 1:
+            grad_copies[step - 1, kind].wait_recv()
+            part = part + gr[step - 2, kind].astype(F32)
+        gs[step - 1, kind] = part.astype(BF16)
+        grad_copies[step, kind] = send(gs.at[step - 1, kind], gr.at[step - 1, kind], g_snd.at[step - 1, kind],
+                                       g_rcv.at[step - 1, kind], preceding)
+
+    mine = chunk_y // 2
     steps_x, steps_y = max(x_len.values()), max(y_len.values())
     for step in range(1, max(steps_x, steps_y, REACH) + 1):
+        if step == 1:
+            conclude(0)
         if step <= steps_x:
-            chain_step("x", step)
+            chain_step("x", 0, step)
+        if step == 1:
+            conclude(1)
         if step <= steps_y:
-            chain_step("y", step)
+            chain_step("y", 0, step)
         if step == 1:
             value_side(REACH)
         if step <= REACH:
-            grad_step(step)
-
+            key_part, value_part = backward(REACH + 1 - step)
+            grad_step(step, 0, key_part)
+        if step <= steps_x:
+            chain_step("x", 1, step)
+        if step <= steps_y:
+            chain_step("y", 1, step)
+        if step <= REACH:
+            grad_step(step, 1, value_part)
+        if step == 1:
+            for half in (0, 1):
+                ya[:, half * 128:(half + 1) * 128] = output_term(y, half)
+            cs[...] = ya[pl.ds(pl.multiple_of((1 - core) * mine, 8), mine), :].astype(BF16)
+            core_copy = send(cs, cr, c_snd, c_rcv, partner)
+
+    key_part, value_part = backward(0)
+    for h in range(HEADS):
+        dq_o[:, h * HEAD:(h + 1) * HEAD] = (query_part[h] * query_scale).T.astype(BF16)
     z_copies = {}
+    za[chunk_x:, :] = jnp.zeros((za.shape[0] - chunk_x, 128), F32)
     for half in (0, 1):
-        za[0:chunk_x, :] = chain_end("x", half)
-        za[chunk_x:, :] = jnp.zeros((za.shape[0] - chunk_x, 128), F32)
+        za[0:chunk_x, :] = weight_end(half)
         for i in range(nz):
             rows = za[i * piece:i * piece + zf.shape[2], :]
             zf[half, i] = rows
@@ -250,30 +288,28 @@
         for o in sorted(range(1, nz), key=lambda o: -min(o, nz - o)):
             z_copies[half, o] = send(zs.at[half, (z + o) % nz], zr.at[half, o - 1], z_snd.at[half, o - 1],
                                      z_rcv.at[half, o - 1], z_peer[o])
-    for half in (0, 1):
-        ya[:, half * 128:(half + 1) * 128] = chain_end("y", half)
-    mine = chunk_y // 2
-    cs[...] = ya[pl.ds(pl.multiple_of((1 - core) * mine, 8), mine), :].astype(BF16)
-    core_copy = send(cs, cr, c_snd, c_rcv, partner)
-
-    key_part, value_part = backward(0)
-    for h in range(HEADS):
-        dq_o[h * HEAD:(h + 1) * HEAD, :] = (query_part[h] * query_scale).astype(BF16)
+    core_copy.wait_recv()
+    output_end(0)
+    output_end(1)
     grad_copies[REACH, 0].wait_recv()
     dk_o[...] = ((key_part + gr[REACH - 1, 0].astype(F32)) * query_scale).astype(BF16)
     grad_copies[REACH, 1].wait_recv()
     dv_o[...] = (value_part + gr[REACH - 1, 1].astype(F32)).astype(BF16)
-    core_copy.wait_recv()
-    out_o[...] = (ya[pl.ds(pl.multiple_of(core * mine, 8), mine), :] + cr[...].astype(F32)).astype(BF16)
     for half in (0, 1):
         part = zf[half, z]
         for o in range(1, nz):
             z_copies[half, o].wait_recv()
             part = part + zr[half, o - 1].astype(F32)
-        dw_o[:, half * 128:(half + 1) * 128] = part
-    for copies in (k_copy, v_copy, chains["x"][-1], chains["y"][-1], grad_copies, z_copies, {0: core_copy}):
+        dw_o[:, half * 128:(half + 1) * 128] = part[:piece]
+    del k_copy[0]
+    for copies in (k_copy, v_copy, chains["x"][-1], chains["y"][-1], grad_copies, last_copies, z_copies, {0: core_copy}):
         for copy in copies.values():
             copy.wait_send()
+
+
+def hand_over(*refs):
+    for src, dst in zip(refs[:5], refs[5:]):
+        dst[...] = src[...]
 
 
 def local(nx, ny, nz, queries, keys, values, out_weight, out_grad, block_doc):
@@ -295,28 +331,38 @@
         V((REACH, 2, size, HEAD), BF16), V((REACH, 2, size, HEAD), BF16),
         V((chunk_x + piece_rows, 128), F32), V((2, nz, piece_rows, 128), F32), V((2, nz, piece_rows, 128), BF16),
         V((2, max(nz - 1, 1), piece_rows, 128), BF16),
-        V((chunk_y, size), F32), V((chunk_y // 2, size), BF16), V((chunk_y // 2, size), BF16),
+        V((chunk_y, size), F32), V((2, 2, 2, chunk_y // 2, 128), BF16), V((2, 2, 2, chunk_y // 2, 128), BF16),
+        V((chunk_y // 2, size), BF16), V((chunk_y // 2, size), BF16),
         DMA((5,)), DMA((REACH,)), DMA((REACH,)), DMA((REACH,)), DMA((REACH,)),
         DMA((x_slots,)), DMA((x_slots,)), DMA((y_slots,)), DMA((y_slots,)),
-        DMA((REACH, 2)), DMA((REACH, 2)), DMA((2, nz - 1)), DMA((2, nz - 1)), DMA, DMA,
+        DMA((REACH, 2)), DMA((REACH, 2)), DMA((2, nz - 1)), DMA((2, nz - 1)),
+        DMA((2, 2, 2)), DMA((2, 2, 2)), DMA, DMA,
     ]
-    anywhere, vmem = pl.BlockSpec(memory_space=pl.ANY), pl.BlockSpec(memory_space=pltpu.VMEM)
-    out, dq, dk, dv, dw = pl.pallas_call(
+    in_hbm, vmem = pl.BlockSpec(memory_space=pltpu.HBM), pl.BlockSpec(memory_space=pltpu.VMEM)
+    results = pl.pallas_call(
         functools.partial(kernel, nx, ny, nz),
         out_shape=[
             jax.ShapeDtypeStruct((chunk_y // 2, size), BF16),
-            jax.ShapeDtypeStruct((width, size), BF16),
+            jax.ShapeDtypeStruct((size, width), BF16),
             jax.ShapeDtypeStruct((size, HEAD), BF16),
             jax.ShapeDtypeStruct((size, HEAD), BF16),
-            jax.ShapeDtypeStruct((piece_rows, width), F32),
+            jax.ShapeDtypeStruct((piece, width), F32),
         ],
-        in_specs=[pl.BlockSpec(memory_space=pltpu.SMEM)] + [anywhere] * 5,
+        in_specs=[pl.BlockSpec(memory_space=pltpu.SMEM)] + [in_hbm] * 5,
         out_specs=[vmem] * 5,
         scratch_shapes=scratch,
-        compiler_params=pltpu.CompilerParams(collective_id=0, has_side_effects=True),
+        compiler_params=pltpu.CompilerParams(collective_id=0, has_side_effects=True, vmem_limit_bytes=40 << 20),
         name="layer",
-    )(block_doc, queries, keys, values, out_weight, out_grad)
-    return out.T, dq.T, dk, dv, dw[:piece].T
+    )(*[pltpu.with_memory_space_constraint(a, pltpu.HBM) for a in (block_doc, queries, keys, values, out_weight, out_grad)])
+    out, dq, dk, dv, dw = pl.pallas_call(
+        hand_over,
+        out_shape=[jax.ShapeDtypeStruct(r.shape, r.dtype) for r in results],
+        in_specs=[vmem] * 5,
+        out_specs=[vmem] * 5,
+        compiler_params=pltpu.CompilerParams(vmem_limit_bytes=8 << 20),
+        name="hand_over",
+    )(*results)
+    return out.T, dq, dk, dv, dw.T
 
 
 def solution(mesh, nx=8, ny=8, nz=8):

time: 74.1 us -> 67.8 us (0.915)
  local copies, waits for them, and re-layouts: 7.56 us -> 0 us
  Pallas kernels: 65.4 us -> 67 us
    unnamed x4 -> x0, local copies, waits for them, and re-layouts: 6.14 us -> none
    transpose x1 -> x0, local copies, waits for them, and re-layouts: 1.42 us -> none  [local(): return (out.T, dq.T, dk, dv, dw[:piece].T)]
    pallas_call x1, Pallas kernels: 65.4 us -> 66.2 us  [local(): pl.pallas_call(functools.partial(kernel, nx, ny, nz), out_shape=[jax.Shap...]
    pallas_call x0 -> x1, Pallas kernels: none -> 0.76 us  [local(): pl.pallas_call(hand_over, out_shape=[jax.ShapeDtypeStruct(r.shape, r.dtyp...]
where the time goes in v2:
time: 67.8 us; the launch traced here: 67.6 us
  Pallas kernels  67 us (99%)
    pallas_call x1, Pallas kernels, local(): pl.pallas_call(functools.partial(kernel, nx, ny, nz), out_shape=[jax.Shap...  66.2 us

profile of v2, /device:TPU:14, one launch (start us, length us, event | category | flops | bytes accessed | tf_op | source)
XLA Modules:
  0.0 67.6 jit_solution(8040224593566324179)
XLA Ops:
  0.6 66.2 %layer.1 = (bf16[168,256]{1,0:T(8,128)(2,1)S(1)}, bf16[256,256]{1,0:T(8,128)(2,1)S(1)}, bf16[256,128]{1,0:T(8,128)(2,1)S(1)}, bf16[256,128]{1,0:T(8,128)(2,1)S(1)}, f32[42,256]{1,0:T(8,128)S(1)}) custom-call(s32[64]{0:T(128)} %doc.1, bf16[256,256]{1,0:T(8,128)(2,1)} %q_in.1, bf16[256,128]{1,0:T(8,128)(2,1)} %k_in.1, bf16[256,128]{1,0:T(8,128)(2,1)} %v_in.1, ...), custom_call_target="tpu_custom_call" | custom-call | tf_op jit(solution)/shard_map/layer/pallas_call | solution.py:342
  66.8 0.8 %hand_over.1 = (bf16[168,256]{1,0:T(8,128)(2,1)}, bf16[256,256]{1,0:T(8,128)(2,1)}, bf16[256,128]{1,0:T(8,128)(2,1)}, bf16[256,128]{1,0:T(8,128)(2,1)}, f32[42,256]{1,0:T(8,128)}) custom-call(bf16[168,256]{1,0:T(8,128)(2,1)S(1)} %get-tuple-element.15.refs_0_, bf16[256,256]{1,0:T(8,128)(2,1)S(1)} %get-tuple-element.16.refs_1_, ...), custom_call_target="tpu_custom_call" | custom-call | tf_op jit(solution)/shard_map/hand_over/pallas_call | solution.py:357

commit v3 on v2

--- a/solution.py
+++ b/solution.py
@@ -35,10 +35,10 @@
     return slot, length
 
 
-def kernel(nx, ny, nz, doc, q_in, k_in, v_in, w_in, g_in, out_o, dq_o, dk_o, dv_o, dw_o, *scratch):
-    (q_s, k_s, v_s, w_s, g_s, wt_s, gt_s, p_s, dp_s, at_s, do_s, dot_s, xs, xr, ys, yr, gs, gr,
-     za, zf, zs, zr, ya, ls, lr, cs, cr,
-     load_sem, k_snd, k_rcv, v_snd, v_rcv, x_snd, x_rcv, y_snd, y_rcv, g_snd, g_rcv, z_snd, z_rcv, l_snd, l_rcv, c_snd, c_rcv) = scratch
+def kernel(nx, ny, nz, doc_in, q_in, k_in, v_in, w_in, g_in, out_o, dq_o, dk_o, dv_o, dw_o, *scratch):
+    (doc, q_s, k_s, v_s, w_s, g_s, wf_s, wt_s, gt_s, p_s, dp_s, at_s, do_s, dot_s, xs, xr, ys, yr, gs, gr,
+     za, zf, zs, zr, cs, cr,
+     load_sem, k_snd, k_rcv, v_snd, v_rcv, x_snd, x_rcv, y_snd, y_rcv, g_snd, g_rcv, z_snd, z_rcv, c_snd, c_rcv, z_ready) = scratch
     n_ctx = nx * nz
     ctx, tp = lax.axis_index("ctx"), lax.axis_index("tp")
     x, z = ctx // nz, ctx % nz
@@ -47,20 +47,19 @@
     x_next = {1: ((x + 1) % nx * nz + z, tp), -1: ((x + nx - 1) % nx * nz + z, tp)}
     y_next = {1: (ctx, (y + 1) % ny * 2 + core), -1: (ctx, (y + ny - 1) % ny * 2 + core)}
     partner = (ctx, y * 2 + 1 - core)
-    y_across = [(ctx, (y + way) % ny * 2 + 1 - core) for way in (1, ny - 1)]
     z_peer = {o: (x * nz + (z + o) % nz, tp) for o in range(1, nz)}
-    chunk_x, chunk_y = gt_s.shape[0] // nx, wt_s.shape[0] // ny
+    chunk_x, chunk_y = gt_s.shape[0] // nx, wt_s.shape[1]
     piece = chunk_x // nz
 
     loads = [pltpu.make_async_copy(src, dst, load_sem.at[i]) for i, (src, dst) in enumerate(
-        [(k_in, k_s.at[0]), (q_in, q_s), (v_in, v_s.at[0]), (g_in, g_s), (w_in, w_s)])]
+        [(k_in, k_s.at[0]), (q_in, q_s), (doc_in, doc), (v_in, v_s.at[0]), (g_in, g_s), (w_in, w_s)])]
     for load in loads:
         load.start()
     barrier = pltpu.get_barrier_semaphore()
-    greeted = [following, preceding, *x_next.values(), *y_next.values(), *y_across, partner, *z_peer.values()]
-    for device in greeted:
+    beside = [*x_next.values(), *y_next.values(), partner]
+    for device in [preceding, *beside]:
         pl.semaphore_signal(barrier, inc=1, device_id=device, device_id_type=MESH)
-    pl.semaphore_wait(barrier, len(greeted))
+    pl.semaphore_wait(barrier, 1 + len(beside))
 
     def send(src, dst, snd, rcv, device):
         copy = pltpu.make_async_remote_copy(src_ref=src, dst_ref=dst, send_sem=snd, recv_sem=rcv, device_id=device,
@@ -77,6 +76,9 @@
         v_copy[d] = send(v_in if d == 0 else v_s.at[d], v_s.at[d + 1], v_snd.at[d], v_rcv.at[d], following)
 
     pass_k(0)
+    pass_v(0)
+    for load in loads[:3]:
+        load.wait()
 
     own_doc = doc[ctx]
     bias = [None] + [
@@ -124,17 +126,12 @@
 
     def turn(src, dst):
         for j in range(src.shape[1] // 128):
-            dst[j * 128:(j + 1) * 128, :] = src[:, j * 128:(j + 1) * 128].T
-
-    for load in loads[:2]:
-        load.wait()
+            dst[j * 128:(j + 1) * 128, :] = src[:, j * 128:(j + 1) * 128].T.astype(dst.dtype)
+
     attend(0)
-    k_copy[0].wait_send()
-    pass_v(0)
-    for load in loads[2:]:
+    for load in loads[3:]:
         load.wait()
     weigh(0)
-    do_s[...] = dot(g_s[...], w_s[...], 1, 1).astype(BF16)
     for d in range(1, REACH + 1):
         k_copy[d - 1].wait_recv()
         if d < REACH:
@@ -144,14 +141,20 @@
         if d < REACH:
             pass_v(d)
             weigh(d)
-            if d == 1:
-                dot_s[...] = dot(w_s[...], g_s[...], 1, 1).astype(BF16)
-                value_side(0)
-            value_side(d)
-            if d == 2:
-                turn(g_s, gt_s)
-            if d == 3:
-                turn(w_s, wt_s)
+        if d == 1:
+            do_s[...] = dot(g_s[...], w_s[...], 1, 1).astype(BF16)
+            dot_s[...] = dot(w_s[...], g_s[...], 1, 1).astype(BF16)
+        if d == 2:
+            turn(g_s, gt_s)
+        if d == 3:
+            turn(w_s, wf_s)
+            for i in range(wt_s.shape[0]):
+                wt_s[i] = wf_s[i * chunk_y:(i + 1) * chunk_y, :].astype(BF16)
+            for block in range(REACH):
+                value_side(block)
+
+    for d in range(1, REACH + 1):
+        pl.semaphore_signal(z_ready, inc=1, device_id=((ctx + n_ctx - d) % n_ctx, tp), device_id_type=MESH)
 
     share, delta = {}, {}
 
@@ -167,61 +170,53 @@
         return dot(rows, at_s[half * 128:(half + 1) * 128, :], 1, 1)
 
     def output_term(at, half):
-        rows = wt_s[pl.ds(pl.multiple_of(at * chunk_y, 16), chunk_y), :]
-        return dot(rows, at_s[:, half * 128:(half + 1) * 128], 1, 0)
+        return dot(wt_s[at * 2 + core], at_s[:, half * 128:(half + 1) * 128], 1, 0)
 
     x_slot, x_len = ring_slots(nx)
     y_slot, y_len = ring_slots(ny)
     chains = {"x": (weight_term, x, nx, x_next, xs, xr, x_snd, x_rcv, x_slot, x_len, {}),
               "y": (output_term, y, ny, y_next, ys, yr, y_snd, y_rcv, y_slot, y_len, {})}
 
-    last_copies = {}
+    core_copies = {}
+
+    def share_terms():
+        for o in sorted(range(ny), key=lambda o: -min(o, ny - o)):
+            cs[o] = dot(wt_s[(y + o) % ny * 2 + 1 - core], at_s[...], 1, 0).astype(BF16)
+            core_copies[o] = send(cs.at[o], cr.at[o], c_snd.at[o], c_rcv.at[o], partner)
+
+    arrived_terms = set()
+
+    def chip_term(o, half):
+        part = output_term((y + o) % ny, half)
+        if o not in arrived_terms:
+            core_copies[o].wait_recv()
+            arrived_terms.add(o)
+        return part + cr[o, :, half * 128:(half + 1) * 128].astype(F32)
 
     def chain_step(name, half, step):
         term, me, n, neighbour, out, arrived, snd, rcv, slot, length, copies = chains[name]
         for way in (1, -1):
             if step > length[half, way]:
                 continue
-            at = (me + n + way * (length[half, way] - step + 1)) % n
-            part = term(at, half)
+            off = way * (length[half, way] - step + 1) % n
+            part = chip_term(off, half) if name == "y" else term((me + off) % n, half)
             if step > 1:
                 before = half, way, step - 1
                 copies[before].wait_recv()
                 part = part + arrived[slot[before]].astype(F32)
-            if name == "y" and step == length[half, way]:
-                side = (1 - way) // 2
-                for to in (0, 1):
-                    ls[half, side, to] = part[to * mine:(to + 1) * mine].astype(BF16)
-                    last_copies[half, side, to] = send(
-                        ls.at[half, side, to], lr.at[half, side, core], l_snd.at[half, side, to],
-                        l_rcv.at[half, side, core], (ctx, (y + ny + way) % ny * 2 + to))
-                continue
             now = slot[half, way, step]
             out[now] = part.astype(BF16)
             copies[half, way, step] = send(out.at[now], arrived.at[now], snd.at[now], rcv.at[now], neighbour[way])
 
-    def weight_end(half):
-        term, me, n, neighbour, out, arrived, snd, rcv, slot, length, copies = chains["x"]
-        part = term(me, half)
+    def chain_end(name, half):
+        term, me, n, neighbour, out, arrived, snd, rcv, slot, length, copies = chains[name]
+        part = chip_term(0, half) if name == "y" else term(me, half)
         for way in (1, -1):
             steps = length[half, way]
             if steps:
                 copies[half, way, steps].wait_recv()
                 part = part + arrived[slot[half, way, steps]].astype(F32)
         return part
-
-    def output_end(half):
-        columns = slice(half * 128, (half + 1) * 128)
-        part = ya[pl.ds(pl.multiple_of(core * mine, 8), mine), columns] + cr[:, columns].astype(F32)
-        for way in (1, -1):
-            if y_len[half, way]:
-                for source in (0, 1):
-                    side = (1 - way) // 2
-                    pltpu.make_async_remote_copy(
-                        src_ref=ls.at[half, side, 0], dst_ref=lr.at[half, side, source], send_sem=l_snd.at[half, side, 0],
-                        recv_sem=l_rcv.at[half, side, source], device_id=partner, device_id_type=MESH).wait_recv()
-                    part = part + lr[half, side, source].astype(F32)
-        out_o[:, columns] = part.astype(BF16)
 
     query_part, grad_copies = {}, {}
 
@@ -246,33 +241,26 @@
         grad_copies[step, kind] = send(gs.at[step - 1, kind], gr.at[step - 1, kind], g_snd.at[step - 1, kind],
                                        g_rcv.at[step - 1, kind], preceding)
 
-    mine = chunk_y // 2
     steps_x, steps_y = max(x_len.values()), max(y_len.values())
-    for step in range(1, max(steps_x, steps_y, REACH) + 1):
+    for step in range(1, max(steps_x, REACH) + 1):
+        for half in (0, 1):
+            if step == 1:
+                conclude(half)
+            if step <= steps_x:
+                chain_step("x", half, step)
+        if step == 2:
+            for o in range(nz // 2 + 1, nz):
+                pl.semaphore_signal(z_ready, inc=1, device_id=z_peer[o], device_id_type=MESH)
         if step == 1:
-            conclude(0)
-        if step <= steps_x:
-            chain_step("x", 0, step)
-        if step == 1:
-            conclude(1)
-        if step <= steps_y:
-            chain_step("y", 0, step)
-        if step == 1:
+            share_terms()
             value_side(REACH)
+        elif step - 1 <= steps_y:
+            for half in (0, 1):
+                chain_step("y", half, step - 1)
         if step <= REACH:
             key_part, value_part = backward(REACH + 1 - step)
             grad_step(step, 0, key_part)
-        if step <= steps_x:
-            chain_step("x", 1, step)
-        if step <= steps_y:
-            chain_step("y", 1, step)
-        if step <= REACH:
             grad_step(step, 1, value_part)
-        if step == 1:
-            for half in (0, 1):
-                ya[:, half * 128:(half + 1) * 128] = output_term(y, half)
-            cs[...] = ya[pl.ds(pl.multiple_of((1 - core) * mine, 8), mine), :].astype(BF16)
-            core_copy = send(cs, cr, c_snd, c_rcv, partner)
 
     key_part, value_part = backward(0)
     for h in range(HEADS):
@@ -280,17 +268,21 @@
     z_copies = {}
     za[chunk_x:, :] = jnp.zeros((za.shape[0] - chunk_x, 128), F32)
     for half in (0, 1):
-        za[0:chunk_x, :] = weight_end(half)
+        za[0:chunk_x, :] = chain_end("x", half)
         for i in range(nz):
             rows = za[i * piece:i * piece + zf.shape[2], :]
             zf[half, i] = rows
             zs[half, i] = rows.astype(BF16)
+        if half == 0:
+            pl.semaphore_wait(z_ready, REACH + nz - 1 - nz // 2)
         for o in sorted(range(1, nz), key=lambda o: -min(o, nz - o)):
             z_copies[half, o] = send(zs.at[half, (z + o) % nz], zr.at[half, o - 1], z_snd.at[half, o - 1],
                                      z_rcv.at[half, o - 1], z_peer[o])
-    core_copy.wait_recv()
-    output_end(0)
-    output_end(1)
+    for step in range(max(steps_x, REACH), steps_y + 1):
+        for half in (0, 1):
+            chain_step("y", half, step)
+    for half in (0, 1):
+        out_o[:, half * 128:(half + 1) * 128] = chain_end("y", half).astype(BF16)
     grad_copies[REACH, 0].wait_recv()
     dk_o[...] = ((key_part + gr[REACH - 1, 0].astype(F32)) * query_scale).astype(BF16)
     grad_copies[REACH, 1].wait_recv()
@@ -301,8 +293,7 @@
             z_copies[half, o].wait_recv()
             part = part + zr[half, o - 1].astype(F32)
         dw_o[:, half * 128:(half + 1) * 128] = part[:piece]
-    del k_copy[0]
-    for copies in (k_copy, v_copy, chains["x"][-1], chains["y"][-1], grad_copies, last_copies, z_copies, {0: core_copy}):
+    for copies in (k_copy, v_copy, chains["x"][-1], chains["y"][-1], grad_copies, z_copies, core_copies):
         for copy in copies.values():
             copy.wait_send()
 
@@ -315,15 +306,17 @@
 def local(nx, ny, nz, queries, keys, values, out_weight, out_grad, block_doc):
     size, width = queries.shape
     features = out_weight.shape[1]
-    chunk_x, chunk_y = features // nx, features // ny
+    chunk_x, chunk_y = features // nx, features // (2 * ny)
     piece = chunk_x // nz
     piece_rows = -(-piece // 16) * 16
     x_slots, y_slots = len(ring_slots(nx)[0]), len(ring_slots(ny)[0])
     DMA = pltpu.SemaphoreType.DMA
     V = pltpu.VMEM
     scratch = [
+        pltpu.SMEM(block_doc.shape, jnp.int32),
         V((size, width), BF16), V((REACH + 1, size, HEAD), BF16), V((REACH + 1, size, HEAD), BF16),
-        V((width, features), BF16), V((size, features), BF16), V((features, width), BF16), V((features, size), BF16),
+        V((width, features), BF16), V((size, features), BF16), V((features, width), F32), V((2 * ny, chunk_y, width), BF16),
+        V((features, size), BF16),
         V((REACH + 1, HEADS, size, size), F32), V((REACH + 1, HEADS, size, size), F32),
         V((width, size), BF16), V((size, width), BF16), V((width, size), BF16),
         V((x_slots, chunk_x, 128), BF16), V((x_slots, chunk_x, 128), BF16),
@@ -331,24 +324,23 @@
         V((REACH, 2, size, HEAD), BF16), V((REACH, 2, size, HEAD), BF16),
         V((chunk_x + piece_rows, 128), F32), V((2, nz, piece_rows, 128), F32), V((2, nz, piece_rows, 128), BF16),
         V((2, max(nz - 1, 1), piece_rows, 128), BF16),
-        V((chunk_y, size), F32), V((2, 2, 2, chunk_y // 2, 128), BF16), V((2, 2, 2, chunk_y // 2, 128), BF16),
-        V((chunk_y // 2, size), BF16), V((chunk_y // 2, size), BF16),
-        DMA((5,)), DMA((REACH,)), DMA((REACH,)), DMA((REACH,)), DMA((REACH,)),
+        V((ny, chunk_y, size), BF16), V((ny, chunk_y, size), BF16),
+        DMA((6,)), DMA((REACH,)), DMA((REACH,)), DMA((REACH,)), DMA((REACH,)),
         DMA((x_slots,)), DMA((x_slots,)), DMA((y_slots,)), DMA((y_slots,)),
-        DMA((REACH, 2)), DMA((REACH, 2)), DMA((2, nz - 1)), DMA((2, nz - 1)),
-        DMA((2, 2, 2)), DMA((2, 2, 2)), DMA, DMA,
+        DMA((REACH, 2)), DMA((REACH, 2)), DMA((2, nz - 1)), DMA((2, nz - 1)), DMA((ny,)), DMA((ny,)),
+        pltpu.SemaphoreType.REGULAR,
     ]
     in_hbm, vmem = pl.BlockSpec(memory_space=pltpu.HBM), pl.BlockSpec(memory_space=pltpu.VMEM)
     results = pl.pallas_call(
         functools.partial(kernel, nx, ny, nz),
         out_shape=[
-            jax.ShapeDtypeStruct((chunk_y // 2, size), BF16),
+            jax.ShapeDtypeStruct((chunk_y, size), BF16),
             jax.ShapeDtypeStruct((size, width), BF16),
             jax.ShapeDtypeStruct((size, HEAD), BF16),
             jax.ShapeDtypeStruct((size, HEAD), BF16),
             jax.ShapeDtypeStruct((piece, width), F32),
         ],
-        in_specs=[pl.BlockSpec(memory_space=pltpu.SMEM)] + [in_hbm] * 5,
+        in_specs=[in_hbm] * 6,
         out_specs=[vmem] * 5,
         scratch_shapes=scratch,
         compiler_params=pltpu.CompilerParams(collective_id=0, has_side_effects=True, vmem_limit_bytes=40 << 20),

time: 67.8 us -> 67 us (0.988); the launches traced: 67.6 us -> 65.8 us
  Pallas kernels: 67 us -> 65.1 us
    pallas_call x1, Pallas kernels: 66.2 us -> 64.4 us  [local(): pl.pallas_call(functools.partial(kernel, nx, ny, nz), out_shape=[jax.Shap...]
where the time goes in v3:
time: 67 us; the launch traced here: 65.8 us
  Pallas kernels  65.1 us (97%)
    pallas_call x1, Pallas kernels, local(): pl.pallas_call(functools.partial(kernel, nx, ny, nz), out_shape=[jax.Shap...  64.4 us

profile of v3, /device:TPU:14, one launch (start us, length us, event | category | flops | bytes accessed | tf_op | source)
XLA Modules:
  0.0 65.8 jit_solution(17881725016199291547)
XLA Ops:
  0.6 64.4 %layer.1 = (bf16[168,256]{1,0:T(8,128)(2,1)S(1)}, bf16[256,256]{1,0:T(8,128)(2,1)S(1)}, bf16[256,128]{1,0:T(8,128)(2,1)S(1)}, bf16[256,128]{1,0:T(8,128)(2,1)S(1)}, f32[42,256]{1,0:T(8,128)S(1)}) custom-call(s32[64]{0:T(128)} %doc_in.1, bf16[256,256]{1,0:T(8,128)(2,1)} %q_in.1, bf16[256,128]{1,0:T(8,128)(2,1)} %k_in.1, bf16[256,128]{1,0:T(8,128)(2,1)} %v_in.1, ...), custom_call_target="tpu_custom_call" | custom-call | tf_op jit(solution)/shard_map/layer/pallas_call | solution.py:334
  65.0 0.8 %hand_over.1 = (bf16[168,256]{1,0:T(8,128)(2,1)}, bf16[256,256]{1,0:T(8,128)(2,1)}, bf16[256,128]{1,0:T(8,128)(2,1)}, bf16[256,128]{1,0:T(8,128)(2,1)}, f32[42,256]{1,0:T(8,128)}) custom-call(bf16[168,256]{1,0:T(8,128)(2,1)S(1)} %get-tuple-element.15.refs_0_, bf16[256,256]{1,0:T(8,128)(2,1)S(1)} %get-tuple-element.16.refs_1_, ...), custom_call_target="tpu_custom_call" | custom-call | tf_op jit(solution)/shard_map/hand_over/pallas_call | solution.py:349
